TPU v7x, 256 devices: a whole 4x4x8 slice. The times are simulated.
256 devices in a mesh: seq: 32 (over x, y, core), mp: 8 (over z).
Axes of the slice: x: 4, y: 4, z: 8, core: 2. Of those that a mesh axis runs over, the one named last changes fastest.
Arguments:
- queries: bfloat16 [4096, 4096], P('seq', 'mp'), may hold values from -2 to 2
- keys: bfloat16 [4096, 4096], P('seq', 'mp'), may hold values from -2 to 2
- values: bfloat16 [4096, 4096], P('seq', 'mp'), may hold values from -6 to 6
- log_decay: float32 [32, 4096], P('mp', 'seq'), may hold values from -1.2 to 0
- residual: bfloat16 [4096, 6144], P(('seq', 'mp')), may hold values from -6 to 6
- out_weight: bfloat16 [4096, 6144], P('mp', 'seq'), may hold values from -0.09375 to 0.09375
- gate_weight: bfloat16 [32, 6144, 2304], P('seq', None, 'mp'), may hold values from -0.078125 to 0.078125
- up_weight: bfloat16 [32, 6144, 2304], P('seq', None, 'mp'), may hold values from -0.078125 to 0.078125
- down_weight: bfloat16 [32, 2304, 6144], P('seq', 'mp'), may hold values from -0.09375 to 0.09375
- expert_ids: int32 [4096, 2], P(('seq', 'mp')), may hold values from 0 to 15, all different within a row; in each aligned block of 16 rows (0 to 15, 16 to 31, ...) at most 3 rows name the same one
- route_weights: float32 [4096, 2], P(('seq', 'mp')), may hold values from 0.2 to 1
Outputs:
- output: bfloat16 [4096, 6144], P(('seq', 'mp'))
Inputs may be any that keep to these rules, and one draw needn't show every extreme that they name: `expert_ids`: the 2 experts of a token differ. Among the 16 tokens of one device (aligned blocks of rows in token order) no expert is named more than 3 times, a bound that some block reaches.
All inputs are finite; a program needn't handle non-finite values.
Results may differ from a plain program's by a relative error of at most 0.015.
Values may be sent and summed in bfloat16 or wider, within the bound.
A program may use at most 128 MiB of HBM per device.

v0:
```python
import jax
import jax.numpy as jnp
from jax import lax
from jax.sharding import PartitionSpec as P

TOP = 2
PAIR = 2


def per_device(
    queries,
    keys,
    values,
    log_decay,
    residual,
    out_weight,
    gate_weight,
    up_weight,
    down_weight,
    expert_ids,
    route_weights,
):
    seq_count = lax.axis_size("seq")
    span_len = queries.shape[0]
    head_count = log_decay.shape[0]
    head_size = queries.shape[1] // head_count
    query_heads = queries.reshape(span_len, head_count, head_size)
    key_heads = keys.reshape(span_len, head_count, head_size)
    value_heads = values.reshape(span_len, head_count, head_size)
    cumulative = jnp.cumsum(log_decay, axis=1)
    positions = jnp.arange(span_len)
    causal = (positions[:, None] >= positions[None, :])[None]
    spread_log = cumulative[:, :, None] - cumulative[:, None, :]
    weight = jnp.where(causal, jnp.exp(jnp.where(causal, spread_log, 0.0)), 0.0)
    raw_scores = jnp.einsum(
        "thd,shd->hts", query_heads, key_heads, preferred_element_type=jnp.float32
    )
    local_scores = (raw_scores * weight).astype(jnp.bfloat16)
    local_part = jnp.einsum(
        "hts,shd->thd", local_scores, value_heads, preferred_element_type=jnp.float32
    )
    span_total = cumulative[:, -1]
    key_scale = jnp.exp(span_total[:, None] - cumulative)
    weighted_keys = (key_scale.T[:, :, None] * key_heads.astype(jnp.float32)).astype(jnp.bfloat16)
    span_state = jnp.einsum(
        "thd,the->hde", weighted_keys, value_heads, preferred_element_type=jnp.float32
    ).astype(jnp.bfloat16)
    decays = lax.all_gather(span_total[None, :], "seq", axis=0, tiled=True)
    running = jnp.cumsum(decays, axis=0)
    my_index = lax.axis_index("seq")
    before = lax.dynamic_index_in_dim(running, jnp.maximum(my_index - 1, 0), 0, keepdims=False)
    shard_piece = lax.all_gather(span_state[None], "seq", axis=0, tiled=True)
    row_count = shard_piece.shape[0]
    source = jnp.arange(row_count)
    earlier_mask = (source < my_index)[:, None]
    factor = jnp.where(
        earlier_mask, jnp.exp(jnp.where(earlier_mask, before[None, :] - running, 0.0)), 0.0
    )
    prefix = jnp.einsum(
        "nh,nhde->hde", factor, shard_piece.astype(jnp.float32), precision=lax.Precision.HIGHEST
    )
    prefix_low = prefix.astype(jnp.bfloat16)
    weighted_queries = (jnp.exp(cumulative).T[:, :, None] * query_heads.astype(jnp.float32)).astype(
        jnp.bfloat16
    )
    carried_part = jnp.einsum(
        "thd,hde->the", weighted_queries, prefix_low, preferred_element_type=jnp.float32
    )
    mixed_heads = local_part + carried_part
    normed = (
        mixed_heads * lax.rsqrt(jnp.mean(mixed_heads * mixed_heads, axis=-1, keepdims=True) + 1e-06)
    ).astype(jnp.bfloat16)
    normed = normed.reshape(span_len, head_count * head_size)
    partial_out = jnp.dot(
        normed,
        lax.all_gather(out_weight, "seq", axis=1, tiled=True),
        preferred_element_type=jnp.float32,
    )
    attn_out = lax.psum_scatter(
        partial_out.astype(jnp.bfloat16), "mp", scatter_dimension=0, tiled=True
    ).astype(jnp.float32)
    hidden_state = (residual.astype(jnp.float32) + attn_out).astype(jnp.bfloat16)
    hidden_wide = hidden_state.astype(jnp.float32)
    moe_input = (
        hidden_wide * lax.rsqrt(jnp.mean(hidden_wide * hidden_wide, axis=-1, keepdims=True) + 1e-06)
    ).astype(jnp.bfloat16)
    model_width = residual.shape[1]
    experts = seq_count // PAIR
    tok_rows = residual.shape[0]
    capacity = max(2, tok_rows * TOP * 3 // (2 * experts))
    assign_count = tok_rows * TOP
    flat_ids = expert_ids.reshape(-1)
    expert_hot = (flat_ids[:, None] == jnp.arange(experts)[None, :]).astype(jnp.int32)
    slot_rank = jnp.sum((jnp.cumsum(expert_hot, axis=0) - expert_hot) * expert_hot, axis=1)
    target = flat_ids * capacity + slot_rank
    slot_hot = (target[:, None] == jnp.arange(experts * capacity)[None, :]).astype(jnp.float32)
    owner_hot = (
        (jnp.arange(assign_count) // TOP)[:, None] == jnp.arange(tok_rows)[None, :]
    ).astype(jnp.float32)
    dispatch_map = jnp.einsum("as,at->st", slot_hot, owner_hot).astype(jnp.bfloat16)
    packed = jnp.dot(dispatch_map, moe_input, preferred_element_type=jnp.float32).astype(
        jnp.bfloat16
    )
    outgoing = jnp.broadcast_to(
        packed.reshape(experts, 1, capacity, model_width), (experts, PAIR, capacity, model_width)
    )
    outgoing = outgoing.reshape(seq_count, capacity, model_width)
    incoming = lax.all_to_all(outgoing, "seq", split_axis=0, concat_axis=0, tiled=True)
    expert_rows = incoming.reshape(seq_count * capacity, model_width)
    gate_matrix = gate_weight[0]
    up_matrix = up_weight[0]
    down_matrix = down_weight[0]
    shard_piece = lax.all_gather(expert_rows, "mp", axis=0, tiled=True)
    gate_value = jnp.dot(shard_piece, gate_matrix, preferred_element_type=jnp.float32)
    lifted = jnp.dot(shard_piece, up_matrix, preferred_element_type=jnp.float32)
    hidden_rows = (jax.nn.silu(gate_value) * lifted).astype(jnp.bfloat16)
    half_out = lax.psum_scatter(
        jnp.dot(hidden_rows, down_matrix, preferred_element_type=jnp.float32).astype(jnp.bfloat16),
        "mp",
        scatter_dimension=0,
        tiled=True,
    )
    returned = lax.all_to_all(
        half_out.reshape(seq_count, capacity, model_width),
        "seq",
        split_axis=0,
        concat_axis=0,
        tiled=True,
    )
    expert_out = jnp.sum(
        returned.reshape(experts, PAIR, capacity, model_width).astype(jnp.float32), axis=1
    )
    expert_out = expert_out.reshape(experts * capacity, model_width)
    weighted = route_weights.reshape(-1)[:, None] * slot_hot
    combine_map = jnp.einsum("at,as->ts", owner_hot, weighted, precision=lax.Precision.HIGHEST)
    expert_mix = jnp.dot(combine_map, expert_out, precision=lax.Precision.HIGHEST)
    return (hidden_wide + expert_mix).astype(jnp.bfloat16)


def solution(mesh):
    placed = (
        P("seq", "mp"),
        P("seq", "mp"),
        P("seq", "mp"),
        P("mp", "seq"),
        P(("seq", "mp"), None),
        P("mp", "seq"),
        P("seq", None, "mp"),
        P("seq", None, "mp"),
        P("seq", "mp", None),
        P(("seq", "mp"), None),
        P(("seq", "mp"), None),
    )
    return jax.shard_map(
        per_device, mesh=mesh, in_specs=placed, out_specs=P(("seq", "mp"), None), check_vma=False
    )
```

profile of v0, /device:TPU:8, one launch (start us, length us, event | category | flops | bytes accessed | tf_op | source)
XLA Modules:
  0.0 483.8 jit_solution(14480048780253203327)
XLA Ops:
  6.5 0.0 copy-start
  6.5 0.0 all-gather.10.cloned.1.call-start
  6.5 1.1 reduce_window_sum.33
  7.7 0.0 copy-start.2
  7.7 0.2 slice_reduce_fusion
  7.9 0.6 exponential_bitcast_fusion.1
  8.5 1.7 copy.40
  10.1 1.8 convolution_convert_fusion.3
  11.9 0.0 all-gather.10.cloned.1.call-update
  11.9 0.0 all-gather.6.cloned.1.call-start
  12.0 0.7 all-gather.6.cloned.1.call-update
  12.7 0.0 reduce-scatter.3.cloned.1.call-start
  12.8 1.3 dynamic-slice
  14.6 0.2 dynamic-update-slice
  14.8 62.4 %all-reduce = f32[128]{0:T(128)S(1)} all-reduce(f32[128]{0:T(128)S(1)} %dynamic-update-slice), channel_id=2, replica_groups=mesh['seq'=32,'mp'=8] {'seq'}, use_global_device_ids=true, to_apply=%add | all-reduce | flops 128 | bytes 1024
  77.2 0.0 copy-done.2
  77.2 0.7 reshape.101
  77.9 0.8 reduce_window_sum.34
  78.7 0.0 copy-start.1
  78.8 0.6 copy-done.1
  79.3 0.6 iota_compare_fusion
  79.9 0.8 select_bitcast_fusion
  80.7 2.2 convolution_bitcast_fusion.1
  82.9 3.7 multiply_reduce_fusion
  86.6 1.7 copy.38
  88.3 1.4 multiply_reduce_fusion.1
  89.7 0.7 multiply_convert_fusion
  90.4 30.7 %all-gather.6.cloned.1.call-done = bf16[512,6144]{0,1:T(8,128)(2,1)} async-done(((bf16[512,192]{0,1:T(8,128)(2,1)}), bf16[512,6144]{0,1:T(8,128)(2,1)}) %all-gather.6.cloned.1.call-update) | async-done | bytes 6291472 | tf_op jit(solution)/shard_map/all_gather | solution.py:76
  121.1 6.2 %convolution_convert_fusion.1 = bf16[128,6144]{1,0:T(8,128)(2,1)} fusion(bf16[128,512]{0,1:T(8,128)(2,1)} %bitcast.79, bf16[512,6144]{0,1:T(8,128)(2,1)} %all-gather.6.cloned.1.call-done), kind=kOutput, calls=%fused_computation.2 | convolution fusion | flops 806092800 | bytes 7995392 | tf_op jit(solution)/shard_map/dot_general | solution.py:74
  127.3 0.0 reduce-scatter.3.cloned.1.call-update
  127.3 0.0 all-gather.8.cloned.1.call-start
  127.4 0.0 copy-done.4
  127.4 0.1 copy.30
  127.5 0.1 reshape.95
  127.6 0.0 copy-start.3
  127.6 0.6 copy-done.3
  128.2 0.7 fusion.49
  128.8 0.8 reduce_window_sum.35
  129.6 0.9 select_reduce_fusion
  130.5 0.7 and_select_fusion
  131.2 36.9 %reduce-scatter.3.cloned.1.call-done = bf16[16,6144]{1,0:T(8,128)(2,1)} async-done(((bf16[128,6144]{1,0:T(8,128)(2,1)}), bf16[16,6144]{1,0:T(8,128)(2,1)}) %reduce-scatter.3.cloned.1.call-update) | async-done | bytes 196624 | tf_op jit(solution)/shard_map/reduce_scatter | solution.py:79
  168.0 1.2 fusion.22
  169.2 2.4 convolution_convert_fusion.2
  171.7 2.1 broadcast_in_dim.65
  173.8 1.9 broadcast_in_dim.66
  175.6 28.6 %all_to_all.10 = bf16[32,3,6144]{2,1,0:T(4,128)(2,1)} all-to-all(bf16[32,3,6144]{2,1,0:T(4,128)(2,1)S(1)} %bitcast.77), channel_id=1, replica_groups=mesh['seq'=32,'mp'=8] {'seq'}, dimensions={0} | all-to-all | bytes 2359296 | tf_op jit(solution)/shard_map/all_to_all | solution.py:108
  204.2 3.9 reshape.97
  208.2 0.0 all-gather.8.cloned.1.call-update
  208.2 0.2 reduce-scatter.5.cloned.1.call-start
  208.4 100.2 %all-gather.8.cloned.1.call-done = bf16[768,6144]{1,0:T(8,128)(2,1)} async-done(((bf16[96,6144]{1,0:T(8,128)(2,1)}), bf16[768,6144]{1,0:T(8,128)(2,1)}) %all-gather.8.cloned.1.call-update) | async-done | bytes 9437200 | tf_op jit(solution)/shard_map/all_gather | solution.py:113
  308.6 8.6 %fusion.4 = f32[768,288]{0,1:T(8,128)} fusion(bf16[768,6144]{1,0:T(8,128)(2,1)} %all-gather.8.cloned.1.call-done, bf16[1,6144,288]{1,2,0:T(8,128)(2,1)} %param.17), kind=kOutput, calls=%fused_computation.9 | convolution fusion | flops 2717908992 | bytes 13860864 | tf_op jit(solution)/shard_map/dot_general | solution.py:114
  317.2 0.0 copy-done
  317.2 15.0 %convolution_convert_fusion = bf16[768,6144]{1,0:T(8,128)(2,1)} fusion(bf16[1,288,6144]{2,1,0:T(8,128)(2,1)S(1)} %copy-done, bf16[768,6144]{1,0:T(8,128)(2,1)} %all-gather.8.cloned.1.call-done, bf16[1,6144,288]{1,2,0:T(8,128)(2,1)} %param.18, f32[768,288]{0,1:T(8,128)} %fusion.4), kind=kOutput, calls=%fused_computation | convolution fusion | flops 5441863680 | bytes 26836992 | tf_op jit(solution)/shard_map/dot_general | solution.py:118
  332.2 0.0 reduce-scatter.5.cloned.1.call-update
  332.2 103.6 %reduce-scatter.5.cloned.1.call-done = bf16[96,6144]{1,0:T(8,128)(2,1)} async-done(((bf16[768,6144]{1,0:T(8,128)(2,1)}), bf16[96,6144]{1,0:T(8,128)(2,1)}) %reduce-scatter.5.cloned.1.call-update) | async-done | bytes 1179664 | tf_op jit(solution)/shard_map/reduce_scatter | solution.py:117
  435.8 3.8 reshape.98
  439.6 7.4 %all-to-all-start.1 = ((bf16[32,3,6144]{2,1,0:T(4,128)(2,1)}), bf16[32,3,6144]{2,1,0:T(4,128)(2,1)}, u32[]{:S(2)}, u32[]{:S(2)}) async-start(bf16[32,3,6144]{2,1,0:T(4,128)(2,1)} %reshape.98), calls=%async_computation.3 | async-start | bytes 3145728 | tf_op jit(solution)/shard_map/all_to_all | solution.py:123
  447.1 0.8 copy.31
  447.8 0.6 mul.82
  448.4 0.9 fusion.47
  449.4 18.7 %all-to-all-done.1 = bf16[32,3,6144]{2,1,0:T(4,128)(2,1)} async-done(((bf16[32,3,6144]{2,1,0:T(4,128)(2,1)}), bf16[32,3,6144]{2,1,0:T(4,128)(2,1)}, u32[]{:S(2)}, u32[]{:S(2)}) %all-to-all-start.1) | async-done | bytes 1179680 | tf_op jit(solution)/shard_map/all_to_all | solution.py:123
  468.1 3.9 convert_reduce_fusion
  471.9 2.5 reshape.99
  474.5 2.7 fusion
  (7 shorter events, 0.0 us)
Async XLA Ops:
  6.5 310.6 %copy-start = (bf16[1,288,6144]{2,1,0:T(8,128)(2,1)S(1)}, bf16[1,288,6144]{2,1,0:T(8,128)(2,1)}, u32[]{:S(2)}) copy-start(bf16[1,288,6144]{2,1,0:T(8,128)(2,1)} %param.19) | copy-start | bytes 10616836
  6.5 76.4 %all-gather.10.cloned.1.call-start = ((), (), s32[]{:S(2)}) async-start(), calls=%async_computation.8 | async-start | bytes 4325376 | tf_op jit(solution)/shard_map/all_gather | solution.py:52
  7.7 69.6 %copy-start.2 = (f32[4,128]{1,0:T(4,128)}, f32[4,128]{1,0:T(4,128)S(1)}, u32[]{:S(2)}) copy-start(f32[4,128]{1,0:T(4,128)S(1)} %reduce_window_sum.33) | copy-start | bytes 6148
  11.9 109.1 %all-gather.6.cloned.1.call-start = ((), (), s32[]{:S(2)}) async-start(), calls=%async_computation.4 | async-start | bytes 6488064 | tf_op jit(solution)/shard_map/all_gather | solution.py:76
  12.7 155.3 %reduce-scatter.3.cloned.1.call-start = ((), (), s32[]{:S(2)}) async-start(), calls=%async_computation.5 | async-start | bytes 1769472 | tf_op jit(solution)/shard_map/reduce_scatter | solution.py:79
  78.7 0.6 copy-start.1
  121.1 6.3 %copy-start.4 = (s32[16,2]{0,1:T(2,128)S(1)}, s32[16,2]{0,1:T(2,128)}, u32[]{:S(2)}) copy-start(s32[16,2]{0,1:T(2,128)} %param.20) | copy-start | bytes 388
  127.3 181.3 %all-gather.8.cloned.1.call-start = ((), (), s32[]{:S(2)}) async-start(), calls=%async_computation.6 | async-start | bytes 10616832 | tf_op jit(solution)/shard_map/all_gather | solution.py:113
  127.6 0.6 copy-start.3
  208.2 227.6 %reduce-scatter.5.cloned.1.call-start = ((), (), s32[]{:S(2)}) async-start(), calls=%async_computation.7 | async-start | bytes 10616832 | tf_op jit(solution)/shard_map/reduce_scatter | solution.py:117
  439.6 28.4 %all-to-all-start.1 = ((bf16[32,3,6144]{2,1,0:T(4,128)(2,1)}), bf16[32,3,6144]{2,1,0:T(4,128)(2,1)}, u32[]{:S(2)}, u32[]{:S(2)}) async-start(bf16[32,3,6144]{2,1,0:T(4,128)(2,1)} %reshape.98), calls=%async_computation.3 | async-start | bytes 3145728 | tf_op jit(solution)/shard_map/all_to_all | solution.py:123
Sparse Core Ops, SparseCore 0:
  12.1 53.6 all-gather.9
  68.3 52.7 all-gather.5
  127.5 40.5 reduce-scatter.2
  208.3 100.2 all-gather.7
  332.4 103.4 reduce-scatter.4
where the time goes:
time: 487 us; the launch traced here: 484 us
  waiting for transfers between devices  291 us (60%)
  blocking collectives  91 us (19%)
  matrix products  41.2 us (8%)
  local copies, waits for them, and re-layouts  22.6 us (5%)
  other arithmetic  16.4 us (3%)
  between operations  13.8 us (3%)
  starting transfers between devices  7.79 us (2%)
    reduce_scatter x1, waiting for transfers between devices, per_device(): lax.psum_scatter(jnp.dot(hidden_rows, down_matrix, preferred_element_type...  104 us
    all_gather x1, waiting for transfers between devices, per_device(): shard_piece = lax.all_gather(expert_rows, 'mp', axis=0, tiled=True)  100 us
    unnamed x1, blocking collectives  62.4 us
    reduce_scatter x1, waiting for transfers between devices, per_device(): lax.psum_scatter(partial_out.astype(jnp.bfloat16), 'mp', scatter_dimensio...  36.9 us
    all_gather x1, waiting for transfers between devices, per_device(): lax.all_gather(out_weight, 'seq', axis=1, tiled=True)  30.7 us
    all_to_all x1, blocking collectives, per_device(): lax.all_to_all(outgoing, 'seq', split_axis=0, concat_axis=0, tiled=True)  28.6 us
    all_to_all x1, waiting for transfers between devices, per_device(): lax.all_to_all(half_out.reshape(seq_count, capacity, model_width), 'seq',...  18.7 us
    dot_general x1, matrix products, per_device(): jnp.dot(hidden_rows, down_matrix, preferred_element_type=jnp.float32)  15 us
  transfers between devices with their start and end apart: 6, of which 5 were waited for; matrix products, arithmetic and copies ran while one was open for 4% of the time, Pallas kernels for 0%

commit v1 on v0

v1 whole, which is shorter than its diff:
```python
import functools

import jax
import jax.numpy as jnp
from jax import lax
from jax.experimental import pallas as pl
from jax.experimental.pallas import tpu as pltpu
from jax.sharding import PartitionSpec as P

MESH = pl.DeviceIdType.MESH
F32 = jnp.float32
BF16 = jnp.bfloat16

SEQ = 32
COLS = 16
NZ = 8
TOK = 128
OWN = 16
HEADS = 4
HD = 128
D = 6144
HALF = D // 2
FG = 288
CAP = 3
ROWS = COLS * CAP
QG = 16
QW = D // QG

RS_LATE = ((3, 1), (4, 0), (3, 0), (2, 1), (2, 0), (1, 1), (1, 0))
RS_PLAIN = ((4, 0), (3, 1), (3, 0), (2, 1), (2, 0), (1, 1), (1, 0))


def dot(a, b):
    return jnp.dot(a, b, preferred_element_type=F32)


def iota(shape, axis):
    return lax.broadcasted_iota(jnp.int32, shape, axis)


def copy_to(src, dst, send, recv, device):
    return pltpu.make_async_remote_copy(
        src_ref=src, dst_ref=dst, send_sem=send, recv_sem=recv, device_id=device, device_id_type=MESH
    )


def kernel(
    q_ref, k_ref, v_ref, ld_ref, res_ref, ow_ref, gate_ref, up_ref, down_ref, ids_ref, rw_ref,
    out_ref,
    st_s, st_r, tot_s, tot_r, pre_s, pre_r, wq_s, loc_s, nrm_s,
    owt_s, ow_s,
    part_s, part_r, hid_s,
    xs_s, d2_s, perm_s, permt_s, g_s, dis_s, dis_r, xg_s,
    gw_s, uw_s, dw_s, acc_s, po_s, po_r, ystk_s, back_s, back_r,
    a2a_sem, lw_sem, sw_send, sw_recv, owx_sem, ring_send, ring_recv, share_send, share_recv,
    rs1_send, rs1_recv, ag_send, ag_recv, rs2_send, rs2_recv,
):
    s = lax.axis_index("seq")
    z = lax.axis_index("mp")
    c = lax.rem(s, 2)
    col = s // 2
    x = col // 4
    y = lax.rem(col, 4)
    other = 1 - c
    sib = {"seq": s + 1 - 2 * c}
    zdev = ({"mp": lax.rem(z + 1, NZ)}, {"mp": lax.rem(z + NZ - 1, NZ)})

    def chip(xx, yy):
        return {"seq": (lax.rem(xx, 4) * 4 + lax.rem(yy, 4)) * 2 + c}

    barrier = pltpu.get_barrier_semaphore()

    def greet(i, carry):
        pl.semaphore_signal(barrier, inc=1, device_id={"seq": lax.rem(s + i, SEQ)}, device_id_type=MESH)
        return carry

    lax.fori_loop(1, SEQ, greet, 0)
    for peer in zdev:
        pl.semaphore_signal(barrier, inc=1, device_id=peer, device_id_type=MESH)

    own_w = [
        pltpu.make_async_copy(gate_ref.at[0], gw_s.at[0], lw_sem.at[0]),
        pltpu.make_async_copy(up_ref.at[0], uw_s.at[0], lw_sem.at[1]),
        pltpu.make_async_copy(down_ref.at[0], dw_s.at[0], lw_sem.at[2]),
    ]
    for cp in own_w:
        cp.start()

    it = iota((TOK, TOK), 0)
    js = iota((TOK, TOK), 1)
    causal = js <= it
    cums = []
    for h in range(HEADS):
        hs = slice(h * HD, (h + 1) * HD)
        row = ld_ref[h : h + 1, :]
        cum_col = jnp.sum(jnp.where(causal, row, 0.0), axis=1, keepdims=True)
        cum_row = jnp.sum(jnp.where(it == js, cum_col, 0.0), axis=0, keepdims=True)
        cums.append((cum_col, cum_row))
        total = cum_row[:, TOK - 1 : TOK]
        wk = (jnp.exp(total - cum_col) * k_ref[:, hs].astype(F32)).astype(BF16)
        state = lax.dot_general(wk, v_ref[:, hs], (((0,), (0,)), ((), ())), preferred_element_type=F32)
        st_s[h * 8 : (h + 1) * 8] = state.astype(BF16).reshape(8, 16, HD)
        tot_s[h] = jnp.broadcast_to(total, (8, HD))
        wq_s[:, hs] = (jnp.exp(cum_col) * q_ref[:, hs].astype(F32)).astype(BF16)

    pl.semaphore_wait(barrier, SEQ - 1 + 2)

    def send_state(i, carry):
        to = lax.rem(s + i, SEQ)
        copy_to(st_s.at[to], st_r.at[s], a2a_sem.at[0], a2a_sem.at[1], {"seq": to}).start()
        copy_to(tot_s.at[to // 8], tot_r.at[s], a2a_sem.at[2], a2a_sem.at[3], {"seq": to}).start()
        return carry

    lax.fori_loop(1, SEQ, send_state, 0)

    owx = copy_to(
        ow_ref.at[pl.ds(pl.multiple_of(other * 256, 256), 256), :], owt_s, owx_sem.at[0], owx_sem.at[1], sib
    )
    owx.start()
    sib_w = [
        copy_to(gate_ref.at[0], gw_s.at[1], sw_send.at[0], sw_recv.at[0], sib),
        copy_to(up_ref.at[0], uw_s.at[1], sw_send.at[1], sw_recv.at[1], sib),
        copy_to(down_ref.at[0], dw_s.at[1], sw_send.at[2], sw_recv.at[2], sib),
    ]
    owx.wait_recv()
    mine = ow_ref[pl.ds(pl.multiple_of(c * 256, 256), 256), :].astype(F32)
    theirs = owt_s[...].astype(F32)
    first = c == 0
    block = jnp.concatenate([jnp.where(first, mine, theirs), jnp.where(first, theirs, mine)], axis=1)
    block = block.astype(BF16).reshape(2, 2, 64, 2 * 192)
    ow_s[c, 0, y, x] = block[0]
    ow_s[c, 1, x, y] = block[1]

    class Ring4:
        def __init__(self, index, get, me, plus, minus):
            before, after = lax.rem(me + 3, 4), lax.rem(me + 1, 4)
            far = lax.rem(me + 2, 4)
            send, recv = ring_send, ring_recv
            own = get(me)
            self.direct = [
                copy_to(own, own, send.at[index, 0], recv.at[index, 0], plus),
                copy_to(own, own, send.at[index, 1], recv.at[index, 1], minus),
            ]
            from_minus, from_plus = get(before).at[0], get(after).at[1]
            self.relay = [
                copy_to(from_minus, from_minus, send.at[index, 2], recv.at[index, 2], plus),
                copy_to(from_plus, from_plus, send.at[index, 3], recv.at[index, 3], minus),
            ]
            self.arrive = [
                copy_to(get(before), get(before), send.at[index, 0], recv.at[index, 0], plus),
                copy_to(get(after), get(after), send.at[index, 1], recv.at[index, 1], minus),
                copy_to(get(far).at[0], get(far).at[0], send.at[index, 2], recv.at[index, 2], plus),
                copy_to(get(far).at[1], get(far).at[1], send.at[index, 3], recv.at[index, 3], minus),
            ]

        def start(self):
            for cp in self.direct:
                cp.start()

        def forward(self):
            for i in range(2):
                self.arrive[i].wait_recv()
                self.relay[i].start()

        def finish(self):
            for i in range(2, 4):
                self.arrive[i].wait_recv()

        def drain(self):
            for cp in self.direct + self.relay:
                cp.wait_send()

    axis_me = ((y, x), (x, y))
    axis_dev = (
        ((chip(x, y + 1), chip(x, y + 3)), (chip(x + 1, y), chip(x + 3, y))),
        ((chip(x + 1, y), chip(x + 3, y)), (chip(x, y + 1), chip(x, y + 3))),
    )
    first_ring = []
    second_ring = [[], []]
    prim_at = [[], []]
    for w in range(2):
        prim, sec = axis_me[w]
        first_ring.append(
            Ring4(w, lambda i, w=w, sec=sec: ow_s.at[c, w, i, sec], prim, *axis_dev[w][0])
        )
        for r in range(4):
            i = lax.rem(prim + r, 4)
            prim_at[w].append(i)
            second_ring[w].append(
                Ring4(2 + w * 4 + r, lambda j, w=w, i=i: ow_s.at[c, w, i, j], sec, *axis_dev[w][1])
            )

    def share(w, r):
        i = prim_at[w][r]
        return copy_to(
            ow_s.at[c, w, i], ow_s.at[c, w, i], share_send.at[w * 4 + r], share_recv.at[w * 4 + r], sib
        )

    for w in range(2):
        first_ring[w].start()
    for w in range(2):
        second_ring[w][0].start()
    for cp in sib_w:
        cp.start()

    for h in range(HEADS):
        hs = slice(h * HD, (h + 1) * HD)
        cum_col, cum_row = cums[h]
        weight = jnp.where(causal, jnp.exp(jnp.where(causal, cum_col - cum_row, 0.0)), 0.0)
        scores = lax.dot_general(
            q_ref[:, hs], k_ref[:, hs], (((1,), (1,)), ((), ())), preferred_element_type=F32
        )
        loc_s[:, hs] = dot((scores * weight).astype(BF16), v_ref[:, hs])

    st_r[s] = st_s[s]
    tot_r[s] = tot_s[s // 8]

    def wait_many(buf, n, sem):
        view = buf.at[pl.ds(0, n)]
        pltpu.make_async_copy(view, view, sem).wait()

    wait_many(st_r, SEQ - 1, a2a_sem.at[1])
    wait_many(tot_r, SEQ - 1, a2a_sem.at[3])
    carry = jnp.zeros((16, HD), F32)
    for b in range(SEQ):
        pre_s[b] = carry.astype(BF16)
        carry = jnp.exp(tot_r[b, 0:1, :]) * carry + st_r[b].astype(F32)

    def send_prefix(i, carry):
        to = lax.rem(s + i, SEQ)
        copy_to(pre_s.at[to], pre_r.at[s], a2a_sem.at[4], a2a_sem.at[5], {"seq": to}).start()
        return carry

    lax.fori_loop(1, SEQ, send_prefix, 0)
    pre_r[s] = pre_s[s]

    for w in range(2):
        first_ring[w].forward()
        second_ring[w][1].start()
        second_ring[w][3].start()
    for w in range(2):
        second_ring[w][0].forward()

    ids = ids_ref[...].astype(F32)
    idc = [ids[:, k : k + 1] for k in range(2)]
    lane_t = lax.bitwise_and(iota((OWN, 256), 1), 15)
    sub_t = iota((OWN, 256), 0)
    idr = [jnp.sum(jnp.where(lane_t == sub_t, idc[k], 0.0), axis=0, keepdims=True) for k in range(2)]
    lane_16 = iota((OWN, 256), 1)
    tgt_row = []
    tgt_col = []
    for k in range(2):
        same = jnp.where(idc[0] == idr[k], 1.0, 0.0) + jnp.where(idc[1] == idr[k], 1.0, 0.0)
        rank = jnp.sum(jnp.where(sub_t < lane_t, same, 0.0), axis=0, keepdims=True)
        tgt_row.append(idr[k] * float(CAP) + rank)
        same = jnp.where(idr[0] == idc[k], 1.0, 0.0) + jnp.where(idr[1] == idc[k], 1.0, 0.0)
        rank = jnp.sum(jnp.where(lane_16 < sub_t, same, 0.0), axis=1, keepdims=True)
        tgt_col.append(jnp.concatenate([idc[k] * float(CAP) + rank] * QG, axis=0))

    ri = iota((768, 256), 0)
    rj = iota((768, 256), 1)
    slot = lax.shift_right_logical(ri, 4).astype(F32)
    hit = ((slot == tgt_row[0]) | (slot == tgt_row[1])) & (
        lax.bitwise_and(ri, 15) == lax.shift_right_logical(rj, 4)
    )
    d2_s[...] = jnp.where(hit, 1.0, 0.0).astype(BF16)
    gi = iota((256, 768), 0)
    gj = iota((256, 768), 1)
    group = lax.shift_right_logical(gi, 4) == lax.bitwise_and(gj, 15)
    slot = lax.shift_right_logical(gj, 4).astype(F32)
    for k in range(2):
        g_s[k] = jnp.where(group & (slot == tgt_col[k]), 1.0, 0.0).astype(BF16)
    pi = iota((768, 768), 0)
    pj = iota((768, 768), 1)
    perm_s[...] = jnp.where(
        pi == lax.bitwise_and(pj, 15) * ROWS + lax.shift_right_logical(pj, 4), 1.0, 0.0
    ).astype(BF16)
    permt_s[...] = jnp.where(
        pj == lax.bitwise_and(pi, 15) * ROWS + lax.shift_right_logical(pi, 4), 1.0, 0.0
    ).astype(BF16)

    wait_many(pre_r, SEQ - 1, a2a_sem.at[5])
    for h in range(HEADS):
        hs = slice(h * HD, (h + 1) * HD)
        prefix = pre_r[h * 8 : (h + 1) * 8].reshape(HD, HD)
        mixed = loc_s[:, hs] + dot(wq_s[:, hs], prefix)
        scale = lax.rsqrt(jnp.mean(mixed * mixed, axis=1, keepdims=True) + 1e-6)
        nrm_s[:, hs] = (mixed * scale).astype(BF16)

    for w in range(2):
        first_ring[w].finish()
        second_ring[w][2].start()
    for w in range(2):
        second_ring[w][1].forward()
        second_ring[w][3].forward()
    for w in range(2):
        second_ring[w][0].finish()
        share(w, 0).start()
    for w in range(2):
        second_ring[w][2].forward()
    for r in (1, 3, 2):
        for w in range(2):
            second_ring[w][r].finish()
            share(w, r).start()
    for w in range(2):
        for r in range(4):
            i = prim_at[w][r]
            copy_to(
                ow_s.at[other, w, i], ow_s.at[other, w, i],
                share_send.at[w * 4 + r], share_recv.at[w * 4 + r], sib,
            ).wait_recv()

    def project(i, carry):
        xx = i // 4
        yy = lax.rem(i, 4)
        total = None
        for cc in range(2):
            rhs = jnp.concatenate(
                [ow_s[cc, 0, yy, xx].reshape(128, 384), ow_s[cc, 1, xx, yy].reshape(128, 384)], axis=0
            )
            term = dot(nrm_s[:, cc * 256 : (cc + 1) * 256], rhs)
            total = term if total is None else total + term
        lanes = pl.ds(pl.multiple_of(lax.rem(i, 8) * QW, QW), QW)
        part_s[:, i // 8, :, lanes] = total.astype(BF16).reshape(NZ, OWN, QW)
        return carry

    lax.fori_loop(0, COLS, project, 0)

    def reduce_steps(own, got, send, recv, order):
        index = {key: i for i, key in enumerate(order)}

        def message(i, way):
            off, h = order[i]
            h = h if way == 0 else 1 - h
            d = lax.rem(z + off, NZ) if way == 0 else lax.rem(z + NZ - off, NZ)
            return own.at[d, h], copy_to(
                own.at[d, h], got.at[way, i], send.at[way, i], recv.at[way, i], zdev[way]
            )

        def arrived(i, way):
            copy_to(
                got.at[way, i], got.at[way, i], send.at[way, i], recv.at[way, i], zdev[way]
            ).wait_recv()
            return got[way, i].astype(F32)

        def step(i):
            off, h = order[i]
            need = index.get((off + 1, h))
            for way in range(2):
                mine, cp = message(i, way)
                if need is not None:
                    mine[...] = (mine[...].astype(F32) + arrived(need, way)).astype(BF16)
                cp.start()

        def result(h):
            total = own[z, h].astype(F32)
            total = total + arrived(index[(1, h)], 0)
            return total + arrived(index[(1, 1 - h)], 1)

        def drain():
            for i in range(len(order)):
                for way in range(2):
                    message(i, way)[1].wait_send()

        return step, result, drain

    rs1_step, rs1_result, rs1_drain = reduce_steps(part_s, part_r, rs1_send, rs1_recv, RS_PLAIN)
    for i in range(7):
        rs1_step(i)

    square = jnp.zeros((OWN, 1), F32)
    for h in (1, 0):
        hid = (res_ref[:, h * HALF : (h + 1) * HALF].astype(F32) + rs1_result(h)).astype(BF16).astype(F32)
        square = square + jnp.sum(hid * hid, axis=1, keepdims=True)
        for g in range(8):
            hid_s[(h * 8 + g) * OWN : (h * 8 + g + 1) * OWN, :] = hid[:, g * QW : (g + 1) * QW]
    scale = lax.rsqrt(square / float(D) + 1e-6)
    scale = jnp.concatenate([scale] * QG, axis=0)
    xs_s[...] = (hid_s[...] * scale).astype(BF16)

    dis_s[...] = dot(d2_s[...], xs_s[...]).astype(BF16).reshape(COLS, ROWS, QW)

    def send_rows(i, carry):
        to = lax.rem(col + i, COLS)
        copy_to(dis_s.at[to], dis_r.at[col], a2a_sem.at[6], a2a_sem.at[7], {"seq": to * 2 + c}).start()
        return carry

    lax.fori_loop(1, COLS, send_rows, 0)
    dis_r[col] = dis_s[col]
    wait_many(dis_r, COLS - 1, a2a_sem.at[7])
    rows = dot(perm_s[...], dis_r[...].reshape(768, QW)).astype(BF16)
    for g in range(QG):
        xg_s[z, g // 8, :, (g % 8) * QW : (g % 8 + 1) * QW] = rows[g * ROWS : (g + 1) * ROWS, :]

    def gather(i, way):
        o = i // 2
        h = i % 2 if way == 0 else 1 - i % 2
        slot = lax.rem(z + NZ - o, NZ) if way == 0 else lax.rem(z + o, NZ)
        ref = xg_s.at[slot, h]
        return copy_to(ref, ref, ag_send.at[way, i], ag_recv.at[way, i], zdev[way])

    def gather_start(i):
        for way in range(2):
            gather(i, way).start()

    def gather_arrive(i):
        o = i // 2
        for way in range(2):
            h = i % 2 if way == 0 else 1 - i % 2
            slot = lax.rem(z + NZ - 1 - o, NZ) if way == 0 else lax.rem(z + o + 1, NZ)
            ref = xg_s.at[slot, h]
            copy_to(ref, ref, ag_send.at[way, i], ag_recv.at[way, i], zdev[way]).wait_recv()

    KC = 768

    def expert(slots):
        m = len(slots) * ROWS
        accs = [acc_s.at[j, pl.ds(0, m), :] for j in range(4)]
        for a in accs:
            a[...] = jnp.zeros((m, FG), F32)

        def lift(i, carry):
            lanes = pl.ds(pl.multiple_of(lax.rem(i, 4) * KC, KC), KC)
            parts = [xg_s[sl, i // 4, :, lanes] for sl in slots]
            left = parts[0] if len(parts) == 1 else jnp.concatenate(parts, axis=0)
            feats = pl.ds(pl.multiple_of(i * KC, KC), KC)
            for j in range(2):
                accs[j][...] += dot(left, gw_s[j, feats, :])
                accs[2 + j][...] += dot(left, uw_s[j, feats, :])
            return carry

        lax.fori_loop(0, D // KC, lift, 0)
        hidden = []
        for j in range(2):
            g = accs[j][...]
            hidden.append((g / (1.0 + jnp.exp(-g)) * accs[2 + j][...]).astype(BF16))

        def lower(i, carry):
            lanes = pl.ds(pl.multiple_of(lax.rem(i, 4) * KC, KC), KC)
            feats = pl.ds(pl.multiple_of(i * KC, KC), KC)
            res = (dot(hidden[0], dw_s[0, :, feats]) + dot(hidden[1], dw_s[1, :, feats])).astype(BF16)
            for n, sl in enumerate(slots):
                po_s[sl, i // 4, :, lanes] = res[n * ROWS : (n + 1) * ROWS, :]
            return carry

        lax.fori_loop(0, D // KC, lower, 0)

    def at(off):
        return lax.rem(z + NZ + off, NZ)

    gather_start(0)
    gather_start(1)
    for cp in own_w:
        cp.wait()
    for cp in sib_w:
        cp.wait_recv()
    expert([z])
    gather_arrive(0)
    gather_start(2)
    gather_arrive(1)
    gather_start(3)
    expert([at(-1), at(1)])
    gather_arrive(2)
    gather_start(4)
    gather_arrive(3)
    gather_start(5)
    expert([at(-2), at(2)])
    gather_arrive(4)
    gather_start(6)
    gather_arrive(5)
    expert([at(-3), at(3)])
    rs2_step, rs2_result, rs2_drain = reduce_steps(po_s, po_r, rs2_send, rs2_recv, RS_LATE)
    rs2_step(0)
    gather_arrive(6)
    expert([at(4)])
    for i in range(1, 7):
        rs2_step(i)

    for h in (1, 0):
        total = rs2_result(h).astype(BF16)
        for g in range(8):
            ystk_s[(h * 8 + g) * ROWS : (h * 8 + g + 1) * ROWS, :] = total[:, g * QW : (g + 1) * QW]
    back_s[...] = dot(permt_s[...], ystk_s[...]).astype(BF16).reshape(COLS, ROWS, QW)

    def send_back(i, carry):
        to = lax.rem(col + i, COLS)
        copy_to(back_s.at[to], back_r.at[col], a2a_sem.at[8], a2a_sem.at[9], {"seq": to * 2 + c}).start()
        return carry

    lax.fori_loop(1, COLS, send_back, 0)
    back_r[col] = back_s[col]
    wait_many(back_r, COLS - 1, a2a_sem.at[9])
    got = back_r[...].reshape(768, QW)
    total = hid_s[...]
    for k in range(2):
        share_k = jnp.concatenate([rw_ref[:, k : k + 1]] * QG, axis=0)
        total = total + share_k * dot(g_s[k], got)
    for g in range(QG):
        out_ref[:, g * QW : (g + 1) * QW] = total[g * OWN : (g + 1) * OWN, :].astype(BF16)

    wait_many(st_s, SEQ - 1, a2a_sem.at[0])
    wait_many(tot_r, SEQ - 1, a2a_sem.at[2])
    wait_many(pre_s, SEQ - 1, a2a_sem.at[4])
    wait_many(dis_s, COLS - 1, a2a_sem.at[6])
    wait_many(back_s, COLS - 1, a2a_sem.at[8])
    owx.wait_send()
    for cp in sib_w:
        cp.wait_send()
    for w in range(2):
        first_ring[w].drain()
        for r in range(4):
            second_ring[w][r].drain()
            share(w, r).wait_send()
    rs1_drain()
    rs2_drain()
    for i in range(7):
        for way in range(2):
            gather(i, way).wait_send()


def layer(queries, keys, values, log_decay, residual, out_weight, gate, up, down, ids, route):
    vmem = pl.BlockSpec(memory_space=pltpu.VMEM)
    hbm = pl.BlockSpec(memory_space=pl.ANY)
    dma = pltpu.SemaphoreType.DMA
    scratch = [
        pltpu.VMEM((SEQ, 16, HD), BF16),
        pltpu.VMEM((SEQ, 16, HD), BF16),
        pltpu.VMEM((HEADS, 8, HD), F32),
        pltpu.VMEM((SEQ, 8, HD), F32),
        pltpu.VMEM((SEQ, 16, HD), BF16),
        pltpu.VMEM((SEQ, 16, HD), BF16),
        pltpu.VMEM((TOK, HEADS * HD), BF16),
        pltpu.VMEM((TOK, HEADS * HD), F32),
        pltpu.VMEM((TOK, HEADS * HD), BF16),
        pltpu.VMEM((256, 192), BF16),
        pltpu.VMEM((2, 2, 4, 4, 2, 64, 384), BF16),
        pltpu.VMEM((NZ, 2, OWN, HALF), BF16),
        pltpu.VMEM((2, 7, OWN, HALF), BF16),
        pltpu.VMEM((QG * OWN, QW), F32),
        pltpu.VMEM((QG * OWN, QW), BF16),
        pltpu.VMEM((768, 256), BF16),
        pltpu.VMEM((768, 768), BF16),
        pltpu.VMEM((768, 768), BF16),
        pltpu.VMEM((2, 256, 768), BF16),
        pltpu.VMEM((COLS, ROWS, QW), BF16),
        pltpu.VMEM((COLS, ROWS, QW), BF16),
        pltpu.VMEM((NZ, 2, ROWS, HALF), BF16),
        pltpu.VMEM((2, D, FG), BF16),
        pltpu.VMEM((2, D, FG), BF16),
        pltpu.VMEM((2, FG, D), BF16),
        pltpu.VMEM((4, 2 * ROWS, FG), F32),
        pltpu.VMEM((NZ, 2, ROWS, HALF), BF16),
        pltpu.VMEM((2, 7, ROWS, HALF), BF16),
        pltpu.VMEM((768, QW), BF16),
        pltpu.VMEM((COLS, ROWS, QW), BF16),
        pltpu.VMEM((COLS, ROWS, QW), BF16),
        dma((10,)),
        dma((3,)),
        dma((3,)),
        dma((3,)),
        dma((2,)),
        dma((10, 4)),
        dma((10, 4)),
        dma((8,)),
        dma((8,)),
        dma((2, 7)),
        dma((2, 7)),
        dma((2, 7)),
        dma((2, 7)),
        dma((2, 7)),
        dma((2, 7)),
    ]
    return pl.pallas_call(
        kernel,
        out_shape=jax.ShapeDtypeStruct((OWN, D), BF16),
        in_specs=[vmem] * 6 + [hbm] * 3 + [vmem] * 2,
        out_specs=vmem,
        scratch_shapes=scratch,
        compiler_params=pltpu.CompilerParams(
            collective_id=0, has_side_effects=True, vmem_limit_bytes=67_000_000
        ),
        name="layer",
    )(queries, keys, values, log_decay, residual, out_weight, gate, up, down, ids, route)


def solution(mesh):
    placed = (
        P("seq", "mp"),
        P("seq", "mp"),
        P("seq", "mp"),
        P("mp", "seq"),
        P(("seq", "mp"), None),
        P("mp", "seq"),
        P("seq", None, "mp"),
        P("seq", None, "mp"),
        P("seq", "mp", None),
        P(("seq", "mp"), None),
        P(("seq", "mp"), None),
    )
    return jax.shard_map(
        layer, mesh=mesh, in_specs=placed, out_specs=P(("seq", "mp"), None), check_vma=False
    )
```

time: 487 us -> 196 us (0.40)
  waiting for transfers between devices: 291 us -> 0 us
  Pallas kernels: 0 us -> 179 us
  blocking collectives: 91 us -> 0 us
  matrix products: 41.2 us -> 0 us
  other arithmetic: 16.4 us -> 0 us
  between operations: 13.8 us -> 0.01 us
  starting transfers between devices: 7.79 us -> 0 us
  local copies, waits for them, and re-layouts: 22.6 us -> 16.6 us
    pallas_call x0 -> x1, Pallas kernels: none -> 179 us  [layer(): pl.pallas_call(kernel, out_shape=jax.ShapeDtypeStruct((OWN, D), BF16), in...]
    reduce_scatter x2 -> x0, waiting for transfers between devices: 140 us -> none  [the longest x1 104 us: per_device(): lax.psum_scatter(jnp.dot(hidden_rows, down_matrix, preferred_element_type...]
    all_gather x3 -> x0, waiting for transfers between devices: 131 us -> none  [the longest x1 100 us: per_device(): shard_piece = lax.all_gather(expert_rows, 'mp', axis=0, tiled=True)]
    unnamed x1 -> x0, blocking collectives: 62.4 us -> none
    dot_general x9 -> x0, matrix products: 41.2 us -> none  [the longest x1 15 us: per_device(): jnp.dot(hidden_rows, down_matrix, preferred_element_type=jnp.float32)]
    all_to_all x1 -> x0, blocking collectives: 28.6 us -> none  [per_device(): lax.all_to_all(outgoing, 'seq', split_axis=0, concat_axis=0, tiled=True)]
    all_to_all x1 -> x0, waiting for transfers between devices: 18.7 us -> none  [per_device(): lax.all_to_all(half_out.reshape(seq_count, capacity, model_width), 'seq',...]
    unnamed x15 -> x8, local copies, waits for them, and re-layouts: 3.51 us -> 16.6 us
  transfers between devices with their start and end apart: 6 -> 0, of which waited for: 5 -> 0; matrix products, arithmetic and copies ran while one was open for 4% -> 0% of each run, Pallas kernels for 0% -> 0%
where the time goes in v1:
time: 196 us
  Pallas kernels  179 us (91%)
  local copies, waits for them, and re-layouts  16.6 us (8%)
    pallas_call x1, Pallas kernels, layer(): pl.pallas_call(kernel, out_shape=jax.ShapeDtypeStruct((OWN, D), BF16), in...  179 us
    unnamed x8, local copies, waits for them, and re-layouts  16.6 us

profile of v1, /device:TPU:8, one launch (start us, length us, event | category | flops | bytes accessed | tf_op | source)
XLA Modules:
  0.0 195.9 jit_solution(377432797893400841)
XLA Ops:
  0.0 1.4 copy.15.ids_ref
  1.4 1.3 copy.16.rw_ref
  2.7 1.8 copy.12.ow_ref
  4.5 0.0 copy-start
  4.5 6.4 %copy.13.gate_ref = bf16[1,6144,288]{2,1,0:T(8,128)(2,1)} copy(bf16[1,6144,288]{1,2,0:T(8,128)(2,1)} %param.17) | data formatting | bytes 7077888 | tf_op args[6]
  10.9 0.0 copy-done
  10.9 4.1 %copy.14.up_ref = bf16[1,6144,288]{2,1,0:T(8,128)(2,1)} copy(bf16[1,6144,288]{1,2,0:T(8,128)(2,1)S(1)} %copy-done) | data formatting | bytes 7077888 | tf_op args[7]
  15.0 179.3 %layer.1 = bf16[16,6144]{1,0:T(8,128)(2,1)} custom-call(bf16[128,512]{1,0:T(8,128)(2,1)} %q_ref.1, bf16[128,512]{1,0:T(8,128)(2,1)} %k_ref.1, bf16[128,512]{1,0:T(8,128)(2,1)} %v_ref.1, f32[4,128]{1,0:T(4,128)} %ld_ref.1, bf16[16,6144]{1,0:T(8,128)(2,1)} %res_ref.1, bf16[512,192]{1,0:T(8,128)(2,1)} %copy.12.ow_ref, bf16[1,6144,288]{2,1,0:T(8,128)(2,1)} %copy.13.gate_ref, ...), custom_call_target="tpu_custom_call" | custom-call | tf_op jit(solution)/shard_map/layer/pallas_call | solution.py:573
  194.3 1.6 copy.18
Async XLA Ops:
  4.5 6.4 %copy-start = (bf16[1,6144,288]{1,2,0:T(8,128)(2,1)S(1)}, bf16[1,6144,288]{1,2,0:T(8,128)(2,1)}, u32[]{:S(2)}) copy-start(bf16[1,6144,288]{1,2,0:T(8,128)(2,1)} %param.18) | copy-start | bytes 10616836

commit v2 on v1

--- a/solution.py
+++ b/solution.py
@@ -34,6 +34,10 @@
     return jnp.dot(a, b, preferred_element_type=F32)
 
 
+def dot_t(a, b):
+    return lax.dot_general(a, b, (((1,), (1,)), ((), ())), preferred_element_type=F32)
+
+
 def iota(shape, axis):
     return lax.broadcasted_iota(jnp.int32, shape, axis)
 
@@ -48,7 +52,7 @@
     q_ref, k_ref, v_ref, ld_ref, res_ref, ow_ref, gate_ref, up_ref, down_ref, ids_ref, rw_ref,
     out_ref,
     st_s, st_r, tot_s, tot_r, pre_s, pre_r, wq_s, loc_s, nrm_s,
-    owt_s, ow_s,
+    ow_s,
     part_s, part_r, hid_s,
     xs_s, d2_s, perm_s, permt_s, g_s, dis_s, dis_r, xg_s,
     gw_s, uw_s, dw_s, acc_s, po_s, po_r, ystk_s, back_s, back_r,
@@ -113,23 +117,34 @@
 
     lax.fori_loop(1, SEQ, send_state, 0)
 
-    owx = copy_to(
-        ow_ref.at[pl.ds(pl.multiple_of(other * 256, 256), 256), :], owt_s, owx_sem.at[0], owx_sem.at[1], sib
-    )
-    owx.start()
+    def lanes_of(core):
+        return pl.ds(pl.multiple_of(core * 256, 256), 256)
+
+    def column_half(core, w):
+        return ow_s.at[core, 0, y, x] if w == 0 else ow_s.at[core, 1, x, y]
+
+    for w in range(2):
+        @pl.when(c == w)
+        def _(w=w):
+            copy_to(
+                ow_ref.at[:, :, lanes_of(other)], column_half(other, w), owx_sem.at[0], owx_sem.at[1], sib
+            ).start()
+            column_half(c, w)[...] = ow_ref[:, :, lanes_of(c)]
+
     sib_w = [
         copy_to(gate_ref.at[0], gw_s.at[1], sw_send.at[0], sw_recv.at[0], sib),
         copy_to(up_ref.at[0], uw_s.at[1], sw_send.at[1], sw_recv.at[1], sib),
         copy_to(down_ref.at[0], dw_s.at[1], sw_send.at[2], sw_recv.at[2], sib),
     ]
-    owx.wait_recv()
-    mine = ow_ref[pl.ds(pl.multiple_of(c * 256, 256), 256), :].astype(F32)
-    theirs = owt_s[...].astype(F32)
-    first = c == 0
-    block = jnp.concatenate([jnp.where(first, mine, theirs), jnp.where(first, theirs, mine)], axis=1)
-    block = block.astype(BF16).reshape(2, 2, 64, 2 * 192)
-    ow_s[c, 0, y, x] = block[0]
-    ow_s[c, 1, x, y] = block[1]
+    def owx(w):
+        return copy_to(
+            ow_ref.at[:, :, lanes_of(other)], column_half(c, 1 - w), owx_sem.at[0], owx_sem.at[1], sib
+        )
+
+    for w in range(2):
+        @pl.when(c == w)
+        def _(w=w):
+            owx(w).wait_recv()
 
     class Ring4:
         def __init__(self, index, get, me, plus, minus):
@@ -242,7 +257,13 @@
         second_ring[w][0].forward()
 
     ids = ids_ref[...].astype(F32)
-    idc = [ids[:, k : k + 1] for k in range(2)]
+    diagonal = iota((OWN, OWN), 0) == iota((OWN, OWN), 1)
+
+    def upright(row):
+        return jnp.sum(jnp.where(diagonal, row, 0.0), axis=1, keepdims=True)
+
+    idc = [upright(ids[k : k + 1, :]) for k in range(2)]
+    share_col = [upright(rw_ref[k : k + 1, :]) for k in range(2)]
     lane_t = lax.bitwise_and(iota((OWN, 256), 1), 15)
     sub_t = iota((OWN, 256), 0)
     idr = [jnp.sum(jnp.where(lane_t == sub_t, idc[k], 0.0), axis=0, keepdims=True) for k in range(2)]
@@ -316,9 +337,9 @@
         total = None
         for cc in range(2):
             rhs = jnp.concatenate(
-                [ow_s[cc, 0, yy, xx].reshape(128, 384), ow_s[cc, 1, xx, yy].reshape(128, 384)], axis=0
+                [ow_s[cc, 0, yy, xx].reshape(192, 256), ow_s[cc, 1, xx, yy].reshape(192, 256)], axis=0
             )
-            term = dot(nrm_s[:, cc * 256 : (cc + 1) * 256], rhs)
+            term = dot_t(nrm_s[:, cc * 256 : (cc + 1) * 256], rhs)
             total = term if total is None else total + term
         lanes = pl.ds(pl.multiple_of(lax.rem(i, 8) * QW, QW), QW)
         part_s[:, i // 8, :, lanes] = total.astype(BF16).reshape(NZ, OWN, QW)
@@ -425,8 +446,8 @@
             left = parts[0] if len(parts) == 1 else jnp.concatenate(parts, axis=0)
             feats = pl.ds(pl.multiple_of(i * KC, KC), KC)
             for j in range(2):
-                accs[j][...] += dot(left, gw_s[j, feats, :])
-                accs[2 + j][...] += dot(left, uw_s[j, feats, :])
+                accs[j][...] += dot_t(left, gw_s[j, :, feats])
+                accs[2 + j][...] += dot_t(left, uw_s[j, :, feats])
             return carry
 
         lax.fori_loop(0, D // KC, lift, 0)
@@ -493,7 +514,7 @@
     got = back_r[...].reshape(768, QW)
     total = hid_s[...]
     for k in range(2):
-        share_k = jnp.concatenate([rw_ref[:, k : k + 1]] * QG, axis=0)
+        share_k = jnp.concatenate([share_col[k]] * QG, axis=0)
         total = total + share_k * dot(g_s[k], got)
     for g in range(QG):
         out_ref[:, g * QW : (g + 1) * QW] = total[g * OWN : (g + 1) * OWN, :].astype(BF16)
@@ -503,7 +524,7 @@
     wait_many(pre_s, SEQ - 1, a2a_sem.at[4])
     wait_many(dis_s, COLS - 1, a2a_sem.at[6])
     wait_many(back_s, COLS - 1, a2a_sem.at[8])
-    owx.wait_send()
+    owx(0).wait_send()
     for cp in sib_w:
         cp.wait_send()
     for w in range(2):
@@ -532,8 +553,7 @@
         pltpu.VMEM((TOK, HEADS * HD), BF16),
         pltpu.VMEM((TOK, HEADS * HD), F32),
         pltpu.VMEM((TOK, HEADS * HD), BF16),
-        pltpu.VMEM((256, 192), BF16),
-        pltpu.VMEM((2, 2, 4, 4, 2, 64, 384), BF16),
+        pltpu.VMEM((2, 2, 4, 4, 2, 96, 256), BF16),
         pltpu.VMEM((NZ, 2, OWN, HALF), BF16),
         pltpu.VMEM((2, 7, OWN, HALF), BF16),
         pltpu.VMEM((QG * OWN, QW), F32),
@@ -545,8 +565,8 @@
         pltpu.VMEM((COLS, ROWS, QW), BF16),
         pltpu.VMEM((COLS, ROWS, QW), BF16),
         pltpu.VMEM((NZ, 2, ROWS, HALF), BF16),
-        pltpu.VMEM((2, D, FG), BF16),
-        pltpu.VMEM((2, D, FG), BF16),
+        pltpu.VMEM((2, FG, D), BF16),
+        pltpu.VMEM((2, FG, D), BF16),
         pltpu.VMEM((2, FG, D), BF16),
         pltpu.VMEM((4, 2 * ROWS, FG), F32),
         pltpu.VMEM((NZ, 2, ROWS, HALF), BF16),
@@ -580,7 +600,10 @@
             collective_id=0, has_side_effects=True, vmem_limit_bytes=67_000_000
         ),
         name="layer",
-    )(queries, keys, values, log_decay, residual, out_weight, gate, up, down, ids, route)
+    )(
+        queries, keys, values, log_decay, residual, out_weight.T.reshape(2, 96, HEADS * HD),
+        jnp.swapaxes(gate, 1, 2), jnp.swapaxes(up, 1, 2), down, ids.T, route.T,
+    )
 
 
 def solution(mesh):

time: 196 us -> 181 us (0.923)
  local copies, waits for them, and re-layouts: 16.6 us -> 1.62 us
    unnamed x8 -> x1, local copies, waits for them, and re-layouts: 16.6 us -> 1.62 us
where the time goes in v2:
time: 181 us
  Pallas kernels  179 us (99%)
    pallas_call x1, Pallas kernels, layer(): pl.pallas_call(kernel, out_shape=jax.ShapeDtypeStruct((OWN, D), BF16), in...  179 us

profile of v2, /device:TPU:8, one launch (start us, length us, event | category | flops | bytes accessed | tf_op | source)
XLA Modules:
  0.0 181.1 jit_solution(6797807996188554029)
XLA Ops:
  0.0 179.5 %layer.1 = bf16[16,6144]{1,0:T(8,128)(2,1)} custom-call(bf16[128,512]{1,0:T(8,128)(2,1)} %q_ref.1, bf16[128,512]{1,0:T(8,128)(2,1)} %k_ref.1, bf16[128,512]{1,0:T(8,128)(2,1)} %v_ref.1, f32[4,128]{1,0:T(4,128)} %ld_ref.1, bf16[16,6144]{1,0:T(8,128)(2,1)} %res_ref.1, bf16[2,96,512]{2,1,0:T(8,128)(2,1)} %bitcast.9, bf16[1,288,6144]{2,1,0:T(8,128)(2,1)} %bitcast.7, ...), custom_call_target="tpu_custom_call" | custom-call | tf_op jit(solution)/shard_map/layer/pallas_call | solution.py:593
  179.5 1.6 copy.13

commit v3 on v2

--- a/solution.py
+++ b/solution.py
@@ -25,6 +25,10 @@
 ROWS = COLS * CAP
 QG = 16
 QW = D // QG
+DA = 4096
+DB = D - DA
+QA = DA // QG
+QB = DB // QG
 
 RS_LATE = ((3, 1), (4, 0), (3, 0), (2, 1), (2, 0), (1, 1), (1, 0))
 RS_PLAIN = ((4, 0), (3, 1), (3, 0), (2, 1), (2, 0), (1, 1), (1, 0))
@@ -53,11 +57,12 @@
     out_ref,
     st_s, st_r, tot_s, tot_r, pre_s, pre_r, wq_s, loc_s, nrm_s,
     ow_s,
-    part_s, part_r, hid_s,
-    xs_s, d2_s, perm_s, permt_s, g_s, dis_s, dis_r, xg_s,
+    part_s, part_r, hid_s, row_s,
+    xs_s, info_s, tgt_s, wgt_s, xb_s, db_s, db_r, d2_s, perm_s, permt_s, g_s, dis_s, dis_r, xg_s,
     gw_s, uw_s, dw_s, acc_s, po_s, po_r, ystk_s, back_s, back_r,
     a2a_sem, lw_sem, sw_send, sw_recv, owx_sem, ring_send, ring_recv, share_send, share_recv,
     rs1_send, rs1_recv, ag_send, ag_recv, rs2_send, rs2_recv,
+    xb_send, xb_recv, db_send, db_recv,
 ):
     s = lax.axis_index("seq")
     z = lax.axis_index("mp")
@@ -79,8 +84,12 @@
         return carry
 
     lax.fori_loop(1, SEQ, greet, 0)
-    for peer in zdev:
-        pl.semaphore_signal(barrier, inc=1, device_id=peer, device_id_type=MESH)
+
+    def greet_z(i, carry):
+        pl.semaphore_signal(barrier, inc=1, device_id={"mp": lax.rem(z + i, NZ)}, device_id_type=MESH)
+        return carry
+
+    lax.fori_loop(1, NZ, greet_z, 0)
 
     own_w = [
         pltpu.make_async_copy(gate_ref.at[0], gw_s.at[0], lw_sem.at[0]),
@@ -107,7 +116,7 @@
         tot_s[h] = jnp.broadcast_to(total, (8, HD))
         wq_s[:, hs] = (jnp.exp(cum_col) * q_ref[:, hs].astype(F32)).astype(BF16)
 
-    pl.semaphore_wait(barrier, SEQ - 1 + 2)
+    pl.semaphore_wait(barrier, SEQ - 1 + NZ - 1)
 
     def send_state(i, carry):
         to = lax.rem(s + i, SEQ)
@@ -215,9 +224,6 @@
         first_ring[w].start()
     for w in range(2):
         second_ring[w][0].start()
-    for cp in sib_w:
-        cp.start()
-
     for h in range(HEADS):
         hs = slice(h * HD, (h + 1) * HD)
         cum_col, cum_row = cums[h]
@@ -226,6 +232,12 @@
             q_ref[:, hs], k_ref[:, hs], (((1,), (1,)), ((), ())), preferred_element_type=F32
         )
         loc_s[:, hs] = dot((scores * weight).astype(BF16), v_ref[:, hs])
+
+    pi = iota((768, 768), 0)
+    pj = iota((768, 768), 1)
+    perm_s[...] = jnp.where(
+        pi == lax.bitwise_and(pj, 15) * ROWS + lax.shift_right_logical(pj, 4), 1.0, 0.0
+    ).astype(BF16)
 
     st_r[s] = st_s[s]
     tot_r[s] = tot_s[s // 8]
@@ -278,27 +290,29 @@
         rank = jnp.sum(jnp.where(lane_16 < sub_t, same, 0.0), axis=1, keepdims=True)
         tgt_col.append(jnp.concatenate([idc[k] * float(CAP) + rank] * QG, axis=0))
 
-    ri = iota((768, 256), 0)
-    rj = iota((768, 256), 1)
-    slot = lax.shift_right_logical(ri, 4).astype(F32)
-    hit = ((slot == tgt_row[0]) | (slot == tgt_row[1])) & (
-        lax.bitwise_and(ri, 15) == lax.shift_right_logical(rj, 4)
-    )
-    d2_s[...] = jnp.where(hit, 1.0, 0.0).astype(BF16)
-    gi = iota((256, 768), 0)
-    gj = iota((256, 768), 1)
-    group = lax.shift_right_logical(gi, 4) == lax.bitwise_and(gj, 15)
-    slot = lax.shift_right_logical(gj, 4).astype(F32)
     for k in range(2):
-        g_s[k] = jnp.where(group & (slot == tgt_col[k]), 1.0, 0.0).astype(BF16)
-    pi = iota((768, 768), 0)
-    pj = iota((768, 768), 1)
-    perm_s[...] = jnp.where(
-        pi == lax.bitwise_and(pj, 15) * ROWS + lax.shift_right_logical(pj, 4), 1.0, 0.0
-    ).astype(BF16)
-    permt_s[...] = jnp.where(
-        pj == lax.bitwise_and(pi, 15) * ROWS + lax.shift_right_logical(pi, 4), 1.0, 0.0
-    ).astype(BF16)
+        tgt_s[k] = jnp.broadcast_to(tgt_col[k], (256, 128))
+        wgt_s[k] = jnp.broadcast_to(jnp.concatenate([share_col[k]] * QG, axis=0), (256, 128))
+
+    info_s[z] = jnp.concatenate(tgt_row + [jnp.zeros((6, 256), F32)], axis=0)
+
+    def send_info(i, carry):
+        to = lax.rem(z + i, NZ)
+        copy_to(info_s.at[z], info_s.at[z], a2a_sem.at[10], a2a_sem.at[11], {"mp": to}).start()
+        return carry
+
+    lax.fori_loop(1, NZ, send_info, 0)
+
+    def slot_map(plane):
+        ri = iota((768, 256), 0)
+        rj = iota((768, 256), 1)
+        slot = lax.shift_right_logical(ri, 4).astype(F32)
+        hit = ((slot == info_s[plane, 0:1, :]) | (slot == info_s[plane, 1:2, :])) & (
+            lax.bitwise_and(ri, 15) == lax.shift_right_logical(rj, 4)
+        )
+        return jnp.where(hit, 1.0, 0.0).astype(BF16)
+
+    d2_s[...] = slot_map(z)
 
     wait_many(pre_r, SEQ - 1, a2a_sem.at[5])
     for h in range(HEADS):
@@ -323,6 +337,8 @@
         for w in range(2):
             second_ring[w][r].finish()
             share(w, r).start()
+    for cp in sib_w:
+        cp.start()
     for w in range(2):
         for r in range(4):
             i = prim_at[w][r]
@@ -395,11 +411,15 @@
         square = square + jnp.sum(hid * hid, axis=1, keepdims=True)
         for g in range(8):
             hid_s[(h * 8 + g) * OWN : (h * 8 + g + 1) * OWN, :] = hid[:, g * QW : (g + 1) * QW]
+        row_s[:, h * HALF : (h + 1) * HALF] = hid
     scale = lax.rsqrt(square / float(D) + 1e-6)
-    scale = jnp.concatenate([scale] * QG, axis=0)
-    xs_s[...] = (hid_s[...] * scale).astype(BF16)
-
-    dis_s[...] = dot(d2_s[...], xs_s[...]).astype(BF16).reshape(COLS, ROWS, QW)
+    for g in range(QG):
+        xs_s[g * OWN : (g + 1) * OWN, :] = (row_s[:, g * QA : (g + 1) * QA] * scale).astype(BF16)
+    for h in range(2):
+        lo = DA + h * (DB // 2)
+        xb_s[z, h] = (row_s[:, lo : lo + DB // 2] * scale).astype(BF16)
+
+    dis_s[...] = dot(d2_s[...], xs_s[...]).astype(BF16).reshape(COLS, ROWS, QA)
 
     def send_rows(i, carry):
         to = lax.rem(col + i, COLS)
@@ -407,32 +427,80 @@
         return carry
 
     lax.fori_loop(1, COLS, send_rows, 0)
+
+    def at(off):
+        return lax.rem(z + NZ + off, NZ)
+
+    def ring_copy(buf, send, recv, i, way, arriving):
+        o = i // 2 + (1 if arriving else 0)
+        h = i % 2 if way == 0 else 1 - i % 2
+        ref = buf.at[at(-o if way == 0 else o), h]
+        return copy_to(ref, ref, send.at[way, i], recv.at[way, i], zdev[way])
+
+    def token_start(i):
+        for way in range(2):
+            ring_copy(xb_s, xb_send, xb_recv, i, way, False).start()
+
+    def token_arrive(i):
+        for way in range(2):
+            ring_copy(xb_s, xb_send, xb_recv, i, way, True).wait_recv()
+
+    def spread(off):
+        plane, n = at(off), off + 3
+        stack = [xb_s[plane, g // 8, :, (g % 8) * QB : (g % 8 + 1) * QB] for g in range(QG)]
+        onehot = d2_s[...] if off == 0 else slot_map(plane)
+        packed = dot(onehot, jnp.concatenate(stack, axis=0)).astype(BF16)
+        db_s[plane] = packed.reshape(COLS, ROWS, QB)
+
+        def send(i, carry):
+            to = lax.rem(col + i, COLS)
+            copy_to(
+                db_s.at[plane, to], db_r.at[plane, col], db_send.at[n], db_recv.at[n], {"seq": to * 2 + c}
+            ).start()
+            return carry
+
+        lax.fori_loop(1, COLS, send, 0)
+
+    def collect(off):
+        plane = at(off)
+        db_r[plane, col] = db_s[plane, col]
+        wait_many(db_r.at[plane], COLS - 1, db_recv.at[off + 3])
+        got = dot(perm_s[...], db_r[plane].reshape(768, QB)).astype(BF16)
+        for g in range(QG):
+            xg_s[plane, 2, :, g * QB : (g + 1) * QB] = got[g * ROWS : (g + 1) * ROWS, :]
+
+    token_start(0)
+    token_start(1)
+    wait_many(info_s, NZ - 1, a2a_sem.at[11])
+    spread(0)
+    token_arrive(0)
+    token_start(2)
+    token_arrive(1)
+    token_start(3)
+    spread(1)
+    spread(-1)
+    token_arrive(2)
+    token_start(4)
+    token_arrive(3)
+    token_start(5)
     dis_r[col] = dis_s[col]
     wait_many(dis_r, COLS - 1, a2a_sem.at[7])
-    rows = dot(perm_s[...], dis_r[...].reshape(768, QW)).astype(BF16)
+    rows = dot(perm_s[...], dis_r[...].reshape(768, QA)).astype(BF16)
     for g in range(QG):
-        xg_s[z, g // 8, :, (g % 8) * QW : (g % 8 + 1) * QW] = rows[g * ROWS : (g + 1) * ROWS, :]
-
-    def gather(i, way):
-        o = i // 2
-        h = i % 2 if way == 0 else 1 - i % 2
-        slot = lax.rem(z + NZ - o, NZ) if way == 0 else lax.rem(z + o, NZ)
-        ref = xg_s.at[slot, h]
-        return copy_to(ref, ref, ag_send.at[way, i], ag_recv.at[way, i], zdev[way])
+        xg_s[z, g // 8, :, (g % 8) * QA : (g % 8 + 1) * QA] = rows[g * ROWS : (g + 1) * ROWS, :]
+    token_arrive(4)
+    token_start(6)
 
     def gather_start(i):
         for way in range(2):
-            gather(i, way).start()
+            ring_copy(xg_s, ag_send, ag_recv, i, way, False).start()
 
     def gather_arrive(i):
-        o = i // 2
         for way in range(2):
-            h = i % 2 if way == 0 else 1 - i % 2
-            slot = lax.rem(z + NZ - 1 - o, NZ) if way == 0 else lax.rem(z + o + 1, NZ)
-            ref = xg_s.at[slot, h]
-            copy_to(ref, ref, ag_send.at[way, i], ag_recv.at[way, i], zdev[way]).wait_recv()
+            ring_copy(xg_s, ag_send, ag_recv, i, way, True).wait_recv()
 
     KC = 768
+    KL = 1024
 
     def expert(slots):
         m = len(slots) * ROWS
@@ -441,16 +509,16 @@
             a[...] = jnp.zeros((m, FG), F32)
 
         def lift(i, carry):
-            lanes = pl.ds(pl.multiple_of(lax.rem(i, 4) * KC, KC), KC)
-            parts = [xg_s[sl, i // 4, :, lanes] for sl in slots]
+            lanes = pl.ds(pl.multiple_of(lax.rem(i, 2) * KL, KL), KL)
+            parts = [xg_s[sl, i // 2, :, lanes] for sl in slots]
             left = parts[0] if len(parts) == 1 else jnp.concatenate(parts, axis=0)
-            feats = pl.ds(pl.multiple_of(i * KC, KC), KC)
+            feats = pl.ds(pl.multiple_of(i * KL, KL), KL)
             for j in range(2):
                 accs[j][...] += dot_t(left, gw_s[j, :, feats])
                 accs[2 + j][...] += dot_t(left, uw_s[j, :, feats])
             return carry
 
-        lax.fori_loop(0, D // KC, lift, 0)
+        lax.fori_loop(0, D // KL, lift, 0)
         hidden = []
         for j in range(2):
             g = accs[j][...]
@@ -466,37 +534,62 @@
 
         lax.fori_loop(0, D // KC, lower, 0)
 
-    def at(off):
-        return lax.rem(z + NZ + off, NZ)
-
     gather_start(0)
     gather_start(1)
+    token_arrive(5)
+    spread(2)
+    spread(-2)
+    token_arrive(6)
+    spread(3)
+    spread(-3)
+    spread(4)
     for cp in own_w:
         cp.wait()
     for cp in sib_w:
         cp.wait_recv()
+    collect(0)
     expert([z])
     gather_arrive(0)
     gather_start(2)
+    collect(1)
+    collect(-1)
     gather_arrive(1)
     gather_start(3)
     expert([at(-1), at(1)])
     gather_arrive(2)
     gather_start(4)
+    collect(2)
+    collect(-2)
     gather_arrive(3)
     gather_start(5)
     expert([at(-2), at(2)])
     gather_arrive(4)
     gather_start(6)
+    collect(3)
+    collect(-3)
+    collect(4)
     gather_arrive(5)
     expert([at(-3), at(3)])
     rs2_step, rs2_result, rs2_drain = reduce_steps(po_s, po_r, rs2_send, rs2_recv, RS_LATE)
     rs2_step(0)
     gather_arrive(6)
     expert([at(4)])
-    for i in range(1, 7):
+    for i in range(1, 5):
         rs2_step(i)
 
+    pi = iota((768, 768), 0)
+    pj = iota((768, 768), 1)
+    permt_s[...] = jnp.where(
+        pj == lax.bitwise_and(pi, 15) * ROWS + lax.shift_right_logical(pi, 4), 1.0, 0.0
+    ).astype(BF16)
+    gi = iota((256, 768), 0)
+    gj = iota((256, 768), 1)
+    group = lax.shift_right_logical(gi, 4) == lax.bitwise_and(gj, 15)
+    slot = lax.shift_right_logical(gj, 4).astype(F32)
+    for k in range(2):
+        g_s[k] = jnp.where(group & (slot == tgt_s[k, :, 0:1]), 1.0, 0.0).astype(BF16)
+    for i in range(5, 7):
+        rs2_step(i)
     for h in (1, 0):
         total = rs2_result(h).astype(BF16)
         for g in range(8):
@@ -514,8 +607,7 @@
     got = back_r[...].reshape(768, QW)
     total = hid_s[...]
     for k in range(2):
-        share_k = jnp.concatenate([share_col[k]] * QG, axis=0)
-        total = total + share_k * dot(g_s[k], got)
+        total = total + wgt_s[k, :, 0:1] * dot(g_s[k], got)
     for g in range(QG):
         out_ref[:, g * QW : (g + 1) * QW] = total[g * OWN : (g + 1) * OWN, :].astype(BF16)
 
@@ -534,9 +626,13 @@
             share(w, r).wait_send()
     rs1_drain()
     rs2_drain()
+    wait_many(info_s, NZ - 1, a2a_sem.at[10])
+    for n in range(NZ):
+        wait_many(db_s.at[0], COLS - 1, db_send.at[n])
     for i in range(7):
         for way in range(2):
-            gather(i, way).wait_send()
+            ring_copy(xb_s, xb_send, xb_recv, i, way, False).wait_send()
+            ring_copy(xg_s, ag_send, ag_recv, i, way, False).wait_send()
 
 
 def layer(queries, keys, values, log_decay, residual, out_weight, gate, up, down, ids, route):
@@ -557,14 +653,21 @@
         pltpu.VMEM((NZ, 2, OWN, HALF), BF16),
         pltpu.VMEM((2, 7, OWN, HALF), BF16),
         pltpu.VMEM((QG * OWN, QW), F32),
-        pltpu.VMEM((QG * OWN, QW), BF16),
+        pltpu.VMEM((OWN, D), F32),
+        pltpu.VMEM((QG * OWN, QA), BF16),
+        pltpu.VMEM((NZ, 8, 256), F32),
+        pltpu.VMEM((2, 256, 128), F32),
+        pltpu.VMEM((2, 256, 128), F32),
+        pltpu.VMEM((NZ, 2, OWN, DB // 2), BF16),
+        pltpu.VMEM((NZ, COLS, ROWS, QB), BF16),
+        pltpu.VMEM((NZ, COLS, ROWS, QB), BF16),
         pltpu.VMEM((768, 256), BF16),
         pltpu.VMEM((768, 768), BF16),
         pltpu.VMEM((768, 768), BF16),
         pltpu.VMEM((2, 256, 768), BF16),
-        pltpu.VMEM((COLS, ROWS, QW), BF16),
-        pltpu.VMEM((COLS, ROWS, QW), BF16),
-        pltpu.VMEM((NZ, 2, ROWS, HALF), BF16),
+        pltpu.VMEM((COLS, ROWS, QA), BF16),
+        pltpu.VMEM((COLS, ROWS, QA), BF16),
+        pltpu.VMEM((NZ, 3, ROWS, DA // 2), BF16),
         pltpu.VMEM((2, FG, D), BF16),
         pltpu.VMEM((2, FG, D), BF16),
         pltpu.VMEM((2, FG, D), BF16),
@@ -574,7 +677,7 @@
         pltpu.VMEM((768, QW), BF16),
         pltpu.VMEM((COLS, ROWS, QW), BF16),
         pltpu.VMEM((COLS, ROWS, QW), BF16),
-        dma((10,)),
+        dma((12,)),
         dma((3,)),
         dma((3,)),
         dma((3,)),
@@ -589,6 +692,10 @@
         dma((2, 7)),
         dma((2, 7)),
         dma((2, 7)),
+        dma((2, 7)),
+        dma((2, 7)),
+        dma((NZ,)),
+        dma((NZ,)),
     ]
     return pl.pallas_call(
         kernel,

time: 181 us -> 173 us (0.956)
  Pallas kernels: 179 us -> 171 us
    pallas_call x1, Pallas kernels: 179 us -> 171 us  [layer(): pl.pallas_call(kernel, out_shape=jax.ShapeDtypeStruct((OWN, D), BF16), in...]
where the time goes in v3:
time: 173 us; the launch traced here: 172 us
  Pallas kernels  171 us (99%)
    pallas_call x1, Pallas kernels, layer(): pl.pallas_call(kernel, out_shape=jax.ShapeDtypeStruct((OWN, D), BF16), in...  171 us

profile of v3, /device:TPU:8, one launch (start us, length us, event | category | flops | bytes accessed | tf_op | source)
XLA Modules:
  0.0 172.2 jit_solution(16966209774486957712)
XLA Ops:
  0.0 170.5 %layer.1 = bf16[16,6144]{1,0:T(8,128)(2,1)} custom-call(bf16[128,512]{1,0:T(8,128)(2,1)} %q_ref.1, bf16[128,512]{1,0:T(8,128)(2,1)} %k_ref.1, bf16[128,512]{1,0:T(8,128)(2,1)} %v_ref.1, f32[4,128]{1,0:T(4,128)} %ld_ref.1, bf16[16,6144]{1,0:T(8,128)(2,1)} %res_ref.1, bf16[2,96,512]{2,1,0:T(8,128)(2,1)} %bitcast.9, bf16[1,288,6144]{2,1,0:T(8,128)(2,1)} %bitcast.7, ...), custom_call_target="tpu_custom_call" | custom-call | tf_op jit(solution)/shard_map/layer/pallas_call | solution.py:700
  170.5 1.6 copy.13
